TPU v7x, 32 devices: a whole 2x2x4 slice. The times are simulated.
32 devices in a mesh: seq: 4 (over x, core), chan: 8 (over z, y).
Axes of the slice: x: 2, y: 2, z: 4, core: 2. Of those that a mesh axis runs over, the one named last changes fastest.
Arguments:
- signal_in: bfloat16 [1024, 8192], P('seq', 'chan'), may hold values from -6 to 6
- gate_in: bfloat16 [1024, 8192], P('seq', 'chan'), may hold values from -6 to 6
- outer_gate: bfloat16 [1024, 8192], P('seq', 'chan'), may hold values from -6 to 6
- cotangent: bfloat16 [1024, 8192], P('seq', 'chan'), may hold values from -6 to 6
- residues: float32 [16, 512], replicated, may hold values from -4 to 4
- log_rates: float32 [16, 512], replicated, may hold values from -11 to -2.5
Outputs:
- grad_signal: bfloat16 [1024, 8192], P('seq', 'chan')
- grad_gate: bfloat16 [1024, 8192], P('seq', 'chan')
- grad_outer: bfloat16 [1024, 8192], P('seq', 'chan')
- grad_residues: float32 [16, 512], replicated
- grad_log_rates: float32 [16, 512], replicated
All inputs are finite; a program needn't handle non-finite values.
Results may differ from a plain program's by a relative error of at most 0.01.
Values may be sent and summed in bfloat16 or wider, within the bound.
A program may use at most 64 MiB of HBM per device.

v0:
```python
import math

import jax
import jax.numpy as jnp
from jax import lax
from jax.sharding import PartitionSpec as P

D = 8192
RADIX = 32


precise = lax.Precision.HIGHEST
full_turn = 2.0 * math.pi


def counting(length):
    return jnp.arange(length, dtype=jnp.int32)


def product(left, right):
    return (left[0] * right[0] - left[1] * right[1], left[0] * right[1] + left[1] * right[0])


def conjugate(pair):
    return (pair[0], -pair[1])


def phases(first, second, modulus, direction):
    angle = full_turn / modulus * (first[:, None] * second[None, :] % modulus).astype(jnp.float32)
    return (jnp.cos(angle), direction * jnp.sin(angle))


def contract(form, matrix, pair):

    def single(left, right):
        return jnp.einsum(form, left, right, precision=precise, preferred_element_type=jnp.float32)

    return (
        single(matrix[0], pair[0]) - single(matrix[1], pair[1]),
        single(matrix[0], pair[1]) + single(matrix[1], pair[0]),
    )


def forward_rows(pair):
    width, rows, cols = pair[0].shape
    inner = rows // RADIX
    shaped = tuple((part.reshape(width, RADIX, inner, cols) for part in pair))
    shaped = contract(
        "ab,wbsc->wasc", phases(counting(RADIX), counting(RADIX), RADIX, -1.0), shaped
    )
    turn = phases(counting(RADIX), counting(inner), rows, -1.0)
    shaped = product(shaped, (turn[0][None, :, :, None], turn[1][None, :, :, None]))
    shaped = contract(
        "ts,wasc->watc", phases(counting(inner), counting(inner), inner, -1.0), shaped
    )
    return tuple((part.reshape(width, rows, cols) for part in shaped))


def inverse_rows(pair):
    width, rows, cols = pair[0].shape
    inner = rows // RADIX
    shaped = tuple((part.reshape(width, RADIX, inner, cols) for part in pair))
    shaped = contract("st,watc->wasc", phases(counting(inner), counting(inner), inner, 1.0), shaped)
    turn = phases(counting(RADIX), counting(inner), rows, 1.0)
    shaped = product(shaped, (turn[0][None, :, :, None], turn[1][None, :, :, None]))
    shaped = contract("ba,wasc->wbsc", phases(counting(RADIX), counting(RADIX), RADIX, 1.0), shaped)
    return tuple((part.reshape(width, rows, cols) for part in shaped))


def row_turn(pair, coarse_rows, rows, period, direction):
    turn = phases(coarse_rows, counting(rows), period, direction)
    return product(pair, (turn[0][:, :, None], turn[1][:, :, None]))


def forward_fold(parts):
    source = counting(parts)
    cosine, sine = phases(source, source, 2 * parts, -1.0)
    alternate = (1 - 2 * (source % 2)).astype(jnp.float32)
    second = jnp.where((source == 0)[:, None], alternate[None, :], sine)
    return jnp.stack([cosine, second], 1)


def inverse_fold(parts, period):
    source = counting(parts)
    cosine, sine = phases(source, source, 2 * parts, 1.0)
    alternate = (1 - 2 * (source % 2)).astype(jnp.float32)[:, None]
    is_first = (source == 0)[None, :]
    first = jnp.where(is_first, 1.0, 2.0 * cosine)
    second = jnp.where(is_first, alternate, -2.0 * sine)
    return jnp.stack([first, second], 1) / period


def frequencies(coarse_rows, rows, parts):
    inner = rows // RADIX
    index = counting(rows)
    fine = index // inner + RADIX * (index % inner)
    return coarse_rows[:, None] + 2 * parts * fine[None, :]


def mode_terms(frequency, period, total, rate):
    angle = full_turn / period * frequency.astype(jnp.float32)
    half_sine = jnp.sin(0.5 * angle)[None, :, :, None]
    sine = jnp.sin(angle)[None, :, :, None]
    odd = (frequency % 2 == 1)[None, :, :, None]
    decay_rate = rate[:, None, None, :]
    decay = jnp.exp(-decay_rate)
    base_real = -jnp.expm1(-decay_rate) + 2.0 * decay * half_sine * half_sine
    base_imaginary = decay * sine
    tail = jnp.exp(-decay_rate * total)
    top = jnp.where(odd, 1.0 + tail, -jnp.expm1(-decay_rate * total))
    size_squared = base_real * base_real + base_imaginary * base_imaginary
    ratio_real = top * base_real / size_squared
    ratio_imaginary = -top * base_imaginary / size_squared
    signed_tail = jnp.where(odd, -tail, tail)
    return (ratio_real, ratio_imaginary, base_real, base_imaginary, size_squared, signed_tail)


def filter_spectrum(frequency, period, total, rate, residue_columns, scale):
    cols = rate.shape[1]
    blank = jnp.zeros(frequency.shape + (cols,), jnp.float32)

    def add_mode(mode, totals):
        rate_row = lax.dynamic_slice_in_dim(rate, mode, 1, 0)
        amplitude = lax.dynamic_slice_in_dim(residue_columns, mode, 1, 0)[:, None, None, :]
        terms = mode_terms(frequency, period, total, rate_row)
        return (
            totals[0] + jnp.sum(amplitude * terms[0], 0),
            totals[1] + jnp.sum(amplitude * terms[1], 0),
        )

    summed = lax.fori_loop(0, rate.shape[0], add_mode, (blank, blank))
    return (scale * summed[0], scale * summed[1])


def spectral_gradients(cross, terms, residue_columns, rate, factor, total):
    ratio_real, ratio_imaginary, base_real, base_imaginary, size_squared, signed_tail = terms
    decay_rate = rate[:, None, None, :]
    shifted = ratio_real - total * signed_tail
    quotient_real = (shifted * base_real + ratio_imaginary * base_imaginary) / size_squared
    quotient_imaginary = (ratio_imaginary * base_real - shifted * base_imaginary) / size_squared
    slope_real = decay_rate * (ratio_real - quotient_real)
    slope_imaginary = decay_rate * (ratio_imaginary - quotient_imaginary)
    cross_real = cross[0][None]
    cross_imaginary = cross[1][None]
    first = factor * jnp.sum(cross_real * ratio_real + cross_imaginary * ratio_imaginary, (1, 2))
    second = (
        factor
        * residue_columns
        * jnp.sum(cross_real * slope_real + cross_imaginary * slope_imaginary, (1, 2))
    )
    return jnp.stack([first, second])


def local_columns(param, start, width, filters):
    if width <= filters:
        return lax.dynamic_slice_in_dim(param, start % filters, width, 1)
    return jnp.tile(param, (1, width // filters))


def place_columns(local, start, filters):
    modes = local.shape[1]
    width = local.shape[2]
    if width <= filters:
        return lax.dynamic_update_slice(
            jnp.zeros((2, modes, filters), jnp.float32), local, (0, 0, start % filters)
        )
    return jnp.sum(local.reshape(2, modes, width // filters, filters), 2)


def on_device(signal_in, gate_in, outer_gate, cotangent, residues, log_rates):
    parts = lax.axis_size("seq")
    position = lax.axis_index("seq")
    group = lax.axis_index("chan")
    rows, cols = signal_in.shape
    total = parts * rows
    period = 2 * total
    slices = rows // parts
    filters = residues.shape[1]
    scale = float(total) ** (-0.5)
    gated = (signal_in.astype(jnp.float32) * gate_in.astype(jnp.float32)).astype(jnp.bfloat16)
    weighted = (cotangent.astype(jnp.float32) * outer_gate.astype(jnp.float32)).astype(jnp.bfloat16)
    start = group * cols
    residue_columns = local_columns(residues, start, cols, filters)
    rate = jnp.exp(local_columns(log_rates, start, cols, filters))
    at_zero = position == 0
    coarse_rows = jnp.stack([position, jnp.where(at_zero, parts, 2 * parts - position)])
    fold_table = forward_fold(parts)
    unfold_table = inverse_fold(parts, period)
    both_inputs = jnp.stack(
        [gated.reshape(parts, slices, cols), weighted.reshape(parts, slices, cols)], 1
    )
    packed = jnp.einsum(
        "epd,dvbc->vepbc",
        fold_table,
        lax.all_to_all(both_inputs, "seq", split_axis=0, concat_axis=0, tiled=True).astype(
            jnp.float32
        ),
        precision=precise,
        preferred_element_type=jnp.float32,
    )
    stacked = lax.all_to_all(packed, "seq", split_axis=1, concat_axis=3, tiled=True)
    results = []
    for which in range(2):
        piece = stacked[which]
        first = piece[0, 0]
        second = piece[0, 1]
        real = jnp.stack([first, jnp.where(at_zero, second, first)])
        imaginary = jnp.stack([jnp.where(at_zero, 0.0, second), jnp.where(at_zero, 0.0, -second)])
        spectrum = forward_rows(row_turn((real, imaginary), coarse_rows, rows, period, -1.0))
        results.append(jnp.stack(spectrum))
    spectra_both = jnp.stack(results)
    gated_pair = (spectra_both[0, 0], spectra_both[0, 1])
    weighted_pair = (spectra_both[1, 0], spectra_both[1, 1])
    frequency = frequencies(coarse_rows, rows, parts)
    cross = product(weighted_pair, conjugate(gated_pair))
    terms = mode_terms(frequency, period, total, rate)
    local = spectral_gradients(cross, terms, residue_columns, rate, scale / period, total)
    filter_pair = filter_spectrum(frequency, period, total, rate, residue_columns, scale)
    spectra = (product(gated_pair, filter_pair), product(weighted_pair, conjugate(filter_pair)))
    sent = []
    for spectrum in spectra:
        back = row_turn(inverse_rows(spectrum), coarse_rows, rows, period, 1.0)
        paired = jnp.stack([back[0][0], jnp.where(at_zero, back[0][1], back[1][0])])
        sent.append(paired.reshape(2, parts, slices, cols))
    settled = jnp.einsum(
        "dpe,npebc->ndbc",
        unfold_table,
        lax.all_to_all(
            jnp.stack(sent).astype(jnp.bfloat16), "seq", split_axis=2, concat_axis=2, tiled=True
        ).astype(jnp.float32),
        precision=precise,
        preferred_element_type=jnp.float32,
    )
    returned = lax.all_to_all(
        settled.astype(jnp.bfloat16), "seq", split_axis=1, concat_axis=2, tiled=True
    ).astype(settled.dtype)
    convolved, grad_gated = tuple(
        (returned[which].reshape(rows, cols) for which in range(len(spectra)))
    )
    totals = lax.psum(place_columns(local, start, filters), ("seq", "chan"))
    norm = float(total * D // filters) ** (-0.5)
    grad_signal = (grad_gated * gate_in.astype(jnp.float32)).astype(jnp.bfloat16)
    grad_gate = (grad_gated * signal_in.astype(jnp.float32)).astype(jnp.bfloat16)
    grad_outer = (cotangent.astype(jnp.float32) * convolved).astype(jnp.bfloat16)
    return (grad_signal, grad_gate, grad_outer, norm * totals[0], norm * totals[1])


def solution(mesh):
    placed = (P("seq", "chan"), P("seq", "chan"), P("seq", "chan"), P("seq", "chan"), P(), P())
    return jax.shard_map(
        on_device,
        mesh=mesh,
        in_specs=placed,
        out_specs=(P("seq", "chan"), P("seq", "chan"), P("seq", "chan"), P(), P()),
        check_vma=False,
    )
```

profile of v0, /device:TPU:1, one launch (start us, length us, event | category | flops | bytes accessed | tf_op | source)
XLA Modules:
  0.0 471.5 jit_solution(14355543078005173933)
XLA Ops:
  11.2 4.3 all-to-all-start
  15.8 12.9 %all-to-all-done = bf16[4,2,64,1024]{3,2,1,0:T(8,128)(2,1)S(1)} async-done(((bf16[4,2,64,1024]{3,2,1,0:T(8,128)(2,1)}), bf16[4,2,64,1024]{3,2,1,0:T(8,128)(2,1)S(1)}, u32[]{:S(2)}, u32[]{:S(2)}) %all-to-all-start) | async-done | bytes 1048608 | tf_op jit(solution)/shard_map/all_to_all | solution.py:195
  32.5 5.3 %copy.109 = f32[2,4,2,64,1024]{4,2,3,0,1:T(2,128)} copy(f32[2,4,2,64,1024]{4,1,2,3,0:T(4,128)S(1)} %convolution_bitcast_fusion) | data formatting | bytes 8388608 | tf_op jit(solution)/shard_map/epd,dvbc->vepbc/transpose | solution.py:192
  37.8 6.0 %all-to-all-start.1 = ((f32[2,4,2,64,1024]{4,2,3,0,1:T(2,128)}), f32[2,4,2,64,1024]{4,2,3,0,1:T(2,128)}, u32[]{:S(2)}, u32[]{:S(2)}) async-start(f32[2,4,2,64,1024]{4,2,3,0,1:T(2,128)} %copy.109), calls=%async_computation.1 | async-start | bytes 8388608 | tf_op jit(solution)/shard_map/all_to_all | solution.py:201
  43.8 67.2 %while.22 = (s32[]{:T(128)}, f32[2,256,1024]{2,1,0:T(8,128)S(1)}, f32[2,256,1024]{2,1,0:T(8,128)}, f32[16,1024]{1,0:T(8,128)S(1)}, f32[16,1024]{1,0:T(8,128)S(1)...) while((s32[]{:T(128)}, f32[2,256,1024]{2,1,0:T(8,128)S(1)}, ...), condition=%wide.region_1.2_spmd.clone.clone.clone, body=%wide.region_0.1_spmd.clone.clone.clone.sunk | while | flops 9976323 | bytes 8461435 | solution.py:131
  47.1 4.0 fusion.451
  51.4 4.0 fusion.451
  55.7 4.0 fusion.451
  60.0 4.0 fusion.451
  64.2 4.0 fusion.451
  68.5 4.0 fusion.451
  72.8 4.0 fusion.451
  77.1 4.0 fusion.451
  81.3 4.0 fusion.451
  89.9 4.0 fusion.451
  98.4 4.0 fusion.451
  107.0 4.0 fusion.451
  143.4 5.4 %fusion.53 = (f32[2,32,8,1024]{3,1,2,0:T(8,128)S(1)}, f32[2,32,8,1024]{3,1,2,0:T(8,128)S(1)}, f32[2,32,8,1024]{3,1,2,0:T(8,128)S(1)}, f32[2,32,8,1024]{3,1,2,0:T(8,128)S(1)}) fusion(f32[2,8,1024,32]{2,3,1,0:T(8,128)S(1)} %fusion.103, f32[32,8]{0,1:T(8,128)S(1)} %get-tuple-element.410, f32[32,8]{0,1:T(8,128)S(1)} %get-tuple-element.411, ...), kind=kOutput, calls=%fused_computation.95 | convolution fusion | flops 208157696 | bytes 18876416 | tf_op jit(solution)/shard_map/ab,wbsc->wasc/dot_general | solution.py:36
  232.5 7.7 %multiply_subtract_fusion.4 = (bf16[2,256,1024]{2,1,0:T(8,128)(2,1)S(1)}, bf16[2,256,1024]{2,1,0:T(8,128)(2,1)S(1)}) fusion(f32[2,256]{1,0:T(2,128)S(1)} %get-tuple-element.402, f32[2,256]{1,0:T(2,128)S(1)} %get-tuple-element.403, f32[2,32,8,1024]{3,1,2,0:T(8,128)S(1)} %subtract_bitcast_fusion.3, f32[2,32,8,1024]{3,1,2,0:T(8,128)S(1)} %add_bitcast_fusion.3, ...), kind=kLoop, calls=%fused_computation.116 | loop fusion | flops 4194304 | bytes 10489856 | tf_op jit(solution)/shard_map/sub | solution.py:21
  251.1 23.2 %all-to-all-done.2 = bf16[2,2,4,64,1024]{4,1,3,0,2:T(2,128)(2,1)S(1)} async-done(((bf16[2,2,4,64,1024]{4,1,3,0,2:T(2,128)(2,1)}), bf16[2,2,4,64,1024]{4,1,3,0,2:T(2,128)(2,1)S(1)}, u32[]{:S(2)}, u32[]{:S(2)}) %all-to-all-start.2) | async-done | bytes 2097184 | tf_op jit(solution)/shard_map/all_to_all | solution.py:228
  274.3 8.3 %fusion.443 = bf16[2,64,1024,4,1]{2,3,1,0,4:T(4,128)(2,1)S(1)} fusion(bf16[2,2,4,64,1024]{4,1,3,0,2:T(2,128)(2,1)S(1)} %all-to-all-done.2, f32[4,2,4,1,1]{0,1,4,3,2:T(2,128)S(1)} %copy.157), kind=kOutput, calls=%fused_computation.519 | convolution fusion | flops 50331648 | bytes 3145856 | tf_op jit(solution)/shard_map/dpe,npebc->ndbc/dot_general | solution.py:225
  284.8 4.5 all-to-all-start.3
  289.3 45.0 %add_reduce_fusion = (f32[16,1024]{1,0:T(8,128)S(1)}, f32[16,1024]{1,0:T(8,128)S(1)}) fusion(f32[2,256,1024]{2,1,0:T(8,128)} %get-tuple-element.342, f32[2,256,1024]{2,1,0:T(8,128)S(1)} %copy-done.1, f32[2,256]{1,0:T(2,128)S(1)} %get-tuple-element.399, f32[16,1024]{1,0:T(8,128)S(1)} %get-tuple-element.383, f32[16,1024]{1,0:T(8,128)S(1)} %get-tuple-element.384, ...), kind=kLoop, calls=%fused_computation.54 | loop fusion | flops 301957120 | bytes 4854272 | tf_op jit(solution)/shard_map/reduce_sum | solution.py:145
  335.9 123.3 %all-reduce.2.cloned.1.call-done = f32[2,16,512]{2,1,0:T(8,128)} async-done(((f32[2,16,512]{2,1,0:T(8,128)}), f32[2,16,512]{2,1,0:T(8,128)}) %all-reduce.2.cloned.1.call-update) | async-done | bytes 65552 | tf_op jit(solution)/shard_map/psum | solution.py:240
  (179 shorter events, 162.5 us)
Async XLA Ops:
  10.1 5.4 %copy-start.6 = (f32[16,512]{1,0:T(8,128)S(1)}, f32[16,512]{1,0:T(8,128)}, u32[]{:S(2)}) copy-start(f32[16,512]{1,0:T(8,128)} %param.13) | copy-start | bytes 98308
  10.1 5.4 %copy-start.5 = (f32[16,512]{1,0:T(8,128)S(1)}, f32[16,512]{1,0:T(8,128)}, u32[]{:S(2)}) copy-start(f32[16,512]{1,0:T(8,128)} %param.12) | copy-start | bytes 98308
  11.2 17.5 %all-to-all-start = ((bf16[4,2,64,1024]{3,2,1,0:T(8,128)(2,1)}), bf16[4,2,64,1024]{3,2,1,0:T(8,128)(2,1)S(1)}, u32[]{:S(2)}, u32[]{:S(2)}) async-start(bf16[4,2,64,1024]{3,2,1,0:T(8,128)(2,1)} %copy.107), calls=%async_computation | async-start | bytes 2097152 | tf_op jit(solution)/shard_map/all_to_all | solution.py:195
  37.8 73.9 %all-to-all-start.1 = ((f32[2,4,2,64,1024]{4,2,3,0,1:T(2,128)}), f32[2,4,2,64,1024]{4,2,3,0,1:T(2,128)}, u32[]{:S(2)}, u32[]{:S(2)}) async-start(f32[2,4,2,64,1024]{4,2,3,0,1:T(2,128)} %copy.109), calls=%async_computation.1 | async-start | bytes 8388608 | tf_op jit(solution)/shard_map/all_to_all | solution.py:201
  175.9 1.6 copy-start
  246.0 28.4 %all-to-all-start.2 = ((bf16[2,2,4,64,1024]{4,1,3,0,2:T(2,128)(2,1)}), bf16[2,2,4,64,1024]{4,1,3,0,2:T(2,128)(2,1)S(1)}, u32[]{:S(2)}, u32[]{:S(2)}) async-start(bf16[2,2,4,64,1024]{4,1,3,0,2:T(2,128)(2,1)} %copy.141), calls=%async_computation.2 | async-start | bytes 4194304 | tf_op jit(solution)/shard_map/all_to_all | solution.py:228
  283.2 6.1 %copy-start.1 = (f32[2,256,1024]{2,1,0:T(8,128)S(1)}, f32[2,256,1024]{2,1,0:T(8,128)}, u32[]{:S(2)}) copy-start(f32[2,256,1024]{2,1,0:T(8,128)} %get-tuple-element.341) | copy-start | bytes 6291460
  284.8 175.7 %all-to-all-start.3 = ((bf16[2,4,64,1024]{3,2,0,1:T(8,128)(2,1)}), bf16[2,4,64,1024]{3,2,0,1:T(8,128)(2,1)S(1)}, u32[]{:S(2)}, u32[]{:S(2)}) async-start(bf16[2,4,64,1024]{3,2,0,1:T(8,128)(2,1)} %copy.144), calls=%async_computation.3 | async-start | bytes 2097152 | tf_op jit(solution)/shard_map/all_to_all | solution.py:234
  289.3 169.9 %all-reduce.2.cloned.1.call-start = ((), (), s32[]{:S(2)}) async-start(), calls=%async_computation.4 | async-start | bytes 131072 | tf_op jit(solution)/shard_map/psum | solution.py:240
  460.8 1.0 copy-start.2
  460.8 1.2 copy-start.3
  461.1 2.2 copy-start.4
Sparse Core Ops, SparseCore 0:
  336.0 123.0 all-reduce.1
where the time goes:
time: 480 us; the launch traced here: 472 us
  waiting for transfers between devices  159 us (33%)
  other arithmetic  138 us (29%)
  matrix products  116 us (24%)
  local copies, waits for them, and re-layouts  24.1 us (5%)
  starting transfers between devices  18.3 us (4%)
  between operations  15.1 us (3%)
    psum x1, waiting for transfers between devices, on_device(): totals = lax.psum(place_columns(local, start, filters), ('seq', 'chan'))  123 us
    dot_general x32, matrix products, single(): jnp.einsum(form, left, right, precision=precise, preferred_element_type=j...  104 us
    add x16, other arithmetic, add_mode(): totals[1] + jnp.sum(amplitude * terms[1], 0)  62.8 us
    reduce_sum x1, other arithmetic, spectral_gradients(): jnp.sum(cross_real * ratio_real + cross_imaginary * ratio_imaginary, (1, 2))  45 us
    all_to_all x1, waiting for transfers between devices, on_device(): lax.all_to_all(jnp.stack(sent).astype(jnp.bfloat16), 'seq', split_axis=2,...  23.2 us
    sub x3, other arithmetic, product(): left[0] * right[0] - left[1] * right[1]  13.5 us
    all_to_all x1, waiting for transfers between devices, on_device(): lax.all_to_all(both_inputs, 'seq', split_axis=0, concat_axis=0, tiled=True)  12.9 us
  transfers between devices with their start and end apart: 5, of which 3 were waited for; matrix products, arithmetic and copies ran while one was open for 25% of the time, Pallas kernels for 0%

commit v1 on v0

v1 whole, which is shorter than its diff:
```python
import functools
import math

import jax
import jax.numpy as jnp
from jax import lax
from jax.experimental import pallas as pl
from jax.experimental.pallas import tpu as pltpu
from jax.sharding import PartitionSpec as P

LANES = 128
SUB = 8
SEG = 16
f32 = jnp.float32


def rows_of(ref, first, stride):
    return ref[pl.ds(first, SUB, stride=stride), :]


def spread(ref, row):
    return jnp.broadcast_to(ref[pl.ds(row, 1), :], (SUB, LANES))


def filter_lanes(block, cols, filters):
    start = lax.axis_index("chan") * cols + block * LANES
    return pl.ds(pl.multiple_of(lax.rem(start, filters), LANES), LANES)


def block_lanes(block):
    return pl.ds(pl.multiple_of(block * LANES, LANES), LANES)


def local_phase(
    scale, sig, gate, outer, cot, res, logr, conv, grad, xs, ys, edge, moment, gsum,
    g_s, w_s, a_s, h_s, pw_s, c_s, d_s, st, lag_s,
):
    rows, cols = sig.shape
    modes, filters = res.shape
    segs = rows // SEG
    groups = segs // SUB

    @pl.loop(0, cols // LANES)
    def _(block):
        lanes = block_lanes(block)
        fl = filter_lanes(block, cols, filters)
        g_s[...] = (sig[:, lanes].astype(f32) * gate[:, lanes].astype(f32)).astype(jnp.bfloat16).astype(f32)
        w_s[...] = (cot[:, lanes].astype(f32) * outer[:, lanes].astype(f32)).astype(jnp.bfloat16).astype(f32)
        rate = jnp.exp(logr[:, fl])
        amp = res[:, fl] * scale
        a = jnp.exp(-rate)
        a_s[...] = a
        power = jnp.ones((modes, LANES), f32)
        for u in range(SEG):
            pw_s[u * modes : (u + 1) * modes, :] = power
            h_s[u : u + 1, :] = jnp.sum(amp * power, 0, keepdims=True)
            power = power * a
        seg_decay = power

        @pl.loop(0, groups)
        def _(group):
            base = group * (SUB * SEG)
            for half in range(0, modes, SUB):
                decay = [spread(a_s, half + k) for k in range(SUB)]
                zero = jnp.zeros((SUB, LANES), f32)
                x, z, y, v = ([zero] * SUB for _ in range(4))
                for j in range(SEG):
                    gj = rows_of(g_s, base + j, SEG)
                    wj = rows_of(w_s, base + SEG - 1 - j, SEG)
                    for k in range(SUB):
                        x[k] = decay[k] * (x[k] + gj)
                        z[k] = decay[k] * z[k] + x[k]
                        t = decay[k] * y[k]
                        y[k] = t + wj
                        v[k] = decay[k] * v[k] + t
                for k in range(SUB):
                    at = pl.ds(pl.multiple_of((half + k) * segs + group * SUB, SUB), SUB)
                    st[0, at, :] = x[k]
                    st[1, at, :] = z[k]
                    st[2, at, :] = y[k]
                    st[3, at, :] = v[k]
            g = [rows_of(g_s, base + j, SEG) for j in range(SEG)]
            w = [rows_of(w_s, base + j, SEG) for j in range(SEG)]
            for u in range(SEG):
                total = w[u] * g[0]
                for j in range(u + 1, SEG):
                    total = total + w[j] * g[j - u]
                lag_s[pl.ds(pl.multiple_of((group * SEG + u) * SUB, SUB), SUB), :] = total
            h = [spread(h_s, u) for u in range(SEG)]
            for j in range(SEG):
                forward = h[0] * g[j]
                for u in range(1, j + 1):
                    forward = forward + h[u] * g[j - u]
                c_s[pl.ds(base + j, SUB, stride=SEG), :] = forward
                backward = h[0] * w[j]
                for u in range(1, SEG - j):
                    backward = backward + h[u] * w[j + u]
                d_s[pl.ds(base + j, SUB, stride=SEG), :] = backward

        conv[:, lanes] = c_s[...]
        grad[:, lanes] = d_s[...]

        gr = jnp.zeros((modes, LANES), f32)
        gl = jnp.zeros((modes, LANES), f32)
        for u in range(SEG):
            total = lag_s[u * SUB : (u + 1) * SUB, :]
            for group in range(1, groups):
                first = (group * SEG + u) * SUB
                total = total + lag_s[first : first + SUB, :]
            term = jnp.sum(total, 0, keepdims=True) * pw_s[u * modes : (u + 1) * modes, :]
            gr = gr + term
            if u > 0:
                gl = gl + float(u) * term
        x = jnp.zeros((modes, LANES), f32)
        xd = x
        for seg in range(segs):
            at = pl.ds(seg, modes, stride=segs)
            e, d, y, v = (st[i, at, :] for i in range(4))
            xs[seg * modes : (seg + 1) * modes, lanes] = x
            if seg > 0:
                gr = gr + x * y
                gl = gl + (xd * y + x * v)
            xd = seg_decay * (xd + float(SEG) * x) + d
            x = seg_decay * x + e
        y = jnp.zeros((modes, LANES), f32)
        yv = y
        for seg in reversed(range(segs)):
            at = pl.ds(seg, modes, stride=segs)
            ys[seg * modes : (seg + 1) * modes, lanes] = y
            yv = st[3, at, :] + seg_decay * (yv + float(SEG) * y)
            y = st[2, at, :] + seg_decay * y
        edge[0, :, lanes] = x
        edge[1, :, lanes] = y
        moment[0, :, lanes] = xd
        moment[1, :, lanes] = yv
        gsum[0, :, lanes] = gr
        gsum[1, :, lanes] = gl


def carried(edges, parts, span, rate, fl_lanes):
    place = lax.axis_index("seq")
    shape = rate.shape
    x0 = jnp.zeros(shape, f32)
    xm = jnp.zeros(shape, f32)
    y0 = jnp.zeros(shape, f32)
    for other in range(parts):
        ahead = jnp.maximum(place - 1 - other, 0).astype(f32) * float(span)
        behind = jnp.maximum(other - place - 1, 0).astype(f32) * float(span)
        e = jnp.where(other < place, edges[other, 0, :, fl_lanes].astype(f32), 0.0) * jnp.exp(-rate * ahead)
        x0 = x0 + e
        xm = xm + ahead * e
        y0 = y0 + jnp.where(other > place, edges[other, 1, :, fl_lanes].astype(f32), 0.0) * jnp.exp(-rate * behind)
    return x0, xm, y0


def gradient_phase(scale, parts, span, edges, edge, moment, gsum, res, logr, totals, carry):
    modes, filters = res.shape
    cols = edge.shape[2]
    totals[...] = jnp.zeros_like(totals)

    @pl.loop(0, cols // LANES)
    def _(block):
        lanes = block_lanes(block)
        fl = filter_lanes(block, cols, filters)
        rate = jnp.exp(logr[:, fl])
        x0, xm, y0 = carried(edges, parts, span, rate, lanes)
        carry[0, :, lanes] = x0
        carry[1, :, lanes] = y0
        w = edge[1, :, lanes]
        gr = gsum[0, :, lanes] + x0 * w
        gl = gsum[1, :, lanes] + x0 * moment[1, :, lanes] + xm * w + moment[0, :, lanes] * y0
        totals[0, :, fl] = totals[0, :, fl] + scale * gr
        totals[1, :, fl] = totals[1, :, fl] - scale * (res[:, fl] * rate) * gl


def output_phase(
    scale, sig, gate, cot, res, logr, conv, grad, xs, ys, carry, out_sig, out_gate, out_outer,
    a_s, c_s, d_s, p_s, q_s,
):
    rows, cols = sig.shape
    modes, filters = res.shape
    segs = rows // SEG
    groups = segs // SUB

    @pl.loop(0, cols // LANES)
    def _(block):
        lanes = block_lanes(block)
        fl = filter_lanes(block, cols, filters)
        rate = jnp.exp(logr[:, fl])
        amp = res[:, fl] * scale
        a_s[...] = jnp.exp(-rate)
        seg_decay = jnp.exp(-rate * float(SEG))
        p = amp * carry[0, :, lanes]
        q = amp * carry[1, :, lanes]
        for seg in range(segs):
            at = slice(seg * modes, (seg + 1) * modes)
            p_s[at, :] = amp * xs[at, lanes] + p
            p = p * seg_decay
            back = segs - 1 - seg
            at = slice(back * modes, (back + 1) * modes)
            q_s[at, :] = amp * ys[at, lanes] + q
            q = q * seg_decay
        c_s[...] = conv[:, lanes]
        d_s[...] = grad[:, lanes]

        @pl.loop(0, groups)
        def _(group):
            base = group * (SUB * SEG)
            for half in range(0, modes, SUB):
                decay = [spread(a_s, half + k) for k in range(SUB)]
                p = [rows_of(p_s, group * (SUB * modes) + half + k, modes) for k in range(SUB)]
                q = [rows_of(q_s, group * (SUB * modes) + half + k, modes) for k in range(SUB)]
                for j in range(SEG):
                    at = pl.ds(base + j, SUB, stride=SEG)
                    c_s[at, :] = c_s[at, :] + tree(p)
                    q = [decay[k] * q[k] for k in range(SUB)]
                    at = pl.ds(base + SEG - 1 - j, SUB, stride=SEG)
                    d_s[at, :] = d_s[at, :] + tree(q)
                    if j < SEG - 1:
                        p = [decay[k] * p[k] for k in range(SUB)]

        d = d_s[...]
        out_sig[:, lanes] = (d * gate[:, lanes].astype(f32)).astype(jnp.bfloat16)
        out_gate[:, lanes] = (d * sig[:, lanes].astype(f32)).astype(jnp.bfloat16)
        out_outer[:, lanes] = (c_s[...] * cot[:, lanes].astype(f32)).astype(jnp.bfloat16)


def tree(values):
    while len(values) > 1:
        values = [values[i] + values[i + 1] for i in range(0, len(values), 2)]
    return values[0]


def finish_phase(scale, parts, span, sig, gate, cot, res, logr, conv, grad, xs, ys, edges, edge, moment, gsum,
                 out_sig, out_gate, out_outer, totals, carry, a_s, c_s, d_s, p_s, q_s):
    gradient_phase(scale, parts, span, edges, edge, moment, gsum, res, logr, totals, carry)
    output_phase(scale, sig, gate, cot, res, logr, conv, grad, xs, ys, carry, out_sig, out_gate, out_outer,
                 a_s, c_s, d_s, p_s, q_s)


def on_device(signal_in, gate_in, outer_gate, cotangent, residues, log_rates):
    parts = lax.axis_size("seq")
    rows, cols = signal_in.shape
    modes, filters = residues.shape
    total = parts * rows
    width = cols * lax.axis_size("chan")
    segs = rows // SEG
    groups = segs // SUB
    scale = float(total) ** (-0.5)
    norm = float(total * width // filters) ** (-0.5)
    whole = pl.BlockSpec(memory_space=pltpu.VMEM)
    shape = jax.ShapeDtypeStruct
    params = pltpu.CompilerParams(vmem_limit_bytes=48 * 1024 * 1024)
    tile = pltpu.VMEM((rows, LANES), f32)
    conv, grad, xs, ys, edge, moment, gsum = pl.pallas_call(
        functools.partial(local_phase, scale),
        out_shape=(
            shape((rows, cols), f32),
            shape((rows, cols), f32),
            shape((segs * modes, cols), f32),
            shape((segs * modes, cols), f32),
            shape((2, modes, cols), f32),
            shape((2, modes, cols), f32),
            shape((2, modes, cols), f32),
        ),
        in_specs=[whole] * 6,
        out_specs=(whole,) * 7,
        scratch_shapes=[
            tile,
            tile,
            pltpu.VMEM((modes, LANES), f32),
            pltpu.VMEM((SEG, LANES), f32),
            pltpu.VMEM((SEG * modes, LANES), f32),
            tile,
            tile,
            pltpu.VMEM((4, modes * segs, LANES), f32),
            pltpu.VMEM((groups * SEG * SUB, LANES), f32),
        ],
        compiler_params=params,
        name="local",
    )(signal_in, gate_in, outer_gate, cotangent, residues, log_rates)
    edges = lax.all_gather(edge, "seq", axis=0)
    out_sig, out_gate, out_outer, totals = pl.pallas_call(
        functools.partial(finish_phase, scale, parts, rows),
        out_shape=(
            shape((rows, cols), jnp.bfloat16),
            shape((rows, cols), jnp.bfloat16),
            shape((rows, cols), jnp.bfloat16),
            shape((2, modes, filters), f32),
        ),
        in_specs=[whole] * 13,
        out_specs=(whole,) * 4,
        scratch_shapes=[
            pltpu.VMEM((2, modes, cols), f32),
            pltpu.VMEM((modes, LANES), f32),
            tile,
            tile,
            pltpu.VMEM((segs * modes, LANES), f32),
            pltpu.VMEM((segs * modes, LANES), f32),
        ],
        compiler_params=params,
        name="finish",
    )(signal_in, gate_in, cotangent, residues, log_rates, conv, grad, xs, ys, edges, edge, moment, gsum)
    totals = norm * lax.psum(totals, ("seq", "chan"))
    return out_sig, out_gate, out_outer, totals[0], totals[1]


def solution(mesh):
    placed = (P("seq", "chan"), P("seq", "chan"), P("seq", "chan"), P("seq", "chan"), P(), P())
    return jax.shard_map(
        on_device,
        mesh=mesh,
        in_specs=placed,
        out_specs=(P("seq", "chan"), P("seq", "chan"), P("seq", "chan"), P(), P()),
        check_vma=False,
    )
```

time: 480 us -> 171 us (0.36)
  the two profiles are of different devices: /device:TPU:1 before, /device:TPU:0 now
where the time goes in v1:
time: 171 us; the launch traced here: 170 us
  waiting for transfers between devices  120 us (70%)
  Pallas kernels  19.2 us (11%)
  between operations  14 us (8%)
  blocking collectives  8.76 us (5%)
  local copies, waits for them, and re-layouts  6.31 us (4%)
    psum x1, waiting for transfers between devices, on_device(): totals = norm * lax.psum(totals, ('seq', 'chan'))  120 us
    pallas_call x1, Pallas kernels, on_device(): pl.pallas_call(functools.partial(local_phase, scale), out_shape=(shape((r...  11.9 us
    all_gather x1, blocking collectives, on_device(): edges = lax.all_gather(edge, 'seq', axis=0)  8.76 us
    pallas_call x1, Pallas kernels, on_device(): pl.pallas_call(functools.partial(finish_phase, scale, parts, rows), out_s...  7.22 us
    unnamed x14, local copies, waits for them, and re-layouts  5.68 us
  transfers between devices with their start and end apart: 1, of which 1 were waited for; matrix products, arithmetic and copies ran while one was open for 0% of the time, Pallas kernels for 0%

profile of v1, /device:TPU:0, one launch (start us, length us, event | category | flops | bytes accessed | tf_op | source)
XLA Modules:
  0.0 169.6 jit_solution(9035552040050347156)
XLA Ops:
  7.2 0.0 all-reduce.2.cloned.1.call-start
  7.2 0.0 copy-start
  7.2 1.0 copy-done
  8.3 0.0 copy-start.1
  8.3 1.0 copy-done.1
  9.3 0.0 copy-start.2
  9.3 1.0 copy-done.2
  10.3 0.0 copy-start.4
  10.3 1.0 copy-done.4
  11.4 0.0 copy-start.5
  11.4 0.8 copy-done.5
  12.1 0.0 copy-start.6
  12.1 0.8 copy-done.6
  12.9 11.9 %local.1 = (f32[256,1024]{1,0:T(8,128)S(1)}, f32[256,1024]{1,0:T(8,128)S(1)}, f32[256,1024]{1,0:T(8,128)S(1)}, f32[256,1024]{1,0:T(8,128)}, f32[2,16,1024]{2,1,0...) custom-call(bf16[256,1024]{1,0:T(8,128)(2,1)S(1)} %copy-done, bf16[256,1024]{1,0:T(8,128)(2,1)S(1)} %copy-done.1, ...), custom_call_target="tpu_custom_call" | custom-call | tf_op jit(solution)/shard_map/local/pallas_call | solution.py:255
  24.8 0.0 copy-start.3
  24.8 8.8 %all-gather = f32[8,16,1024]{2,1,0:T(8,128)S(1)} all-gather(f32[2,16,1024]{2,1,0:T(8,128)S(1)} %get-tuple-element.20.edge), channel_id=2, replica_groups=mesh['seq'=4,'chan'=8] {'seq'}, dimensions={0}, use_global_device_ids=true | all-gather | bytes 655360 | tf_op jit(solution)/shard_map/all_gather | solution.py:282
  33.6 0.0 copy-done.3
  33.6 7.2 %finish.1 = (bf16[256,1024]{1,0:T(8,128)(2,1)}, bf16[256,1024]{1,0:T(8,128)(2,1)}, bf16[256,1024]{1,0:T(8,128)(2,1)}, f32[2,16,512]{2,1,0:T(8,128)}) custom-call(bf16[256,1024]{1,0:T(8,128)(2,1)S(1)} %copy-done, bf16[256,1024]{1,0:T(8,128)(2,1)S(1)} %copy-done.1, bf16[256,1024]{1,0:T(8,128)(2,1)S(1)} %copy-done.3, f32[16,512]{1,0:T(8,128)S(1)} %copy-done.5, ...), custom_call_target="tpu_custom_call" | custom-call | tf_op jit(solution)/shard_map/finish/pallas_call | solution.py:283
  40.8 0.0 all-reduce.2.cloned.1.call-update
  40.8 120.4 %all-reduce.2.cloned.1.call-done = f32[2,16,512]{2,1,0:T(8,128)} async-done(((f32[2,16,512]{2,1,0:T(8,128)}), f32[2,16,512]{2,1,0:T(8,128)}) %all-reduce.2.cloned.1.call-update) | async-done | bytes 65552 | tf_op jit(solution)/shard_map/psum | solution.py:304
  161.2 0.8 broadcast_multiply_fusion
  162.1 0.6 slice_bitcast_fusion
Async XLA Ops:
  7.2 154.1 %all-reduce.2.cloned.1.call-start = ((), (), s32[]{:S(2)}) async-start(), calls=%async_computation | async-start | bytes 131072 | tf_op jit(solution)/shard_map/psum | solution.py:304
  7.2 1.0 copy-start
  8.3 1.0 copy-start.1
  9.3 1.0 copy-start.2
  10.3 1.0 copy-start.4
  11.4 0.8 copy-start.5
  12.1 0.8 copy-start.6
  24.8 8.8 %copy-start.3 = (bf16[256,1024]{1,0:T(8,128)(2,1)S(1)}, bf16[256,1024]{1,0:T(8,128)(2,1)}, u32[]{:S(2)}) copy-start(bf16[256,1024]{1,0:T(8,128)(2,1)} %cot.3) | copy-start | bytes 1572868
Sparse Core Ops, SparseCore 0:
  41.0 120.2 all-reduce.1

commit v2 on v0

v2 whole, which is shorter than its diff:
```python
import functools
import math

import jax
import jax.numpy as jnp
from jax import lax
from jax.experimental import pallas as pl
from jax.experimental.pallas import tpu as pltpu
from jax.sharding import PartitionSpec as P

LANES = 128
SUB = 8
SEG = 16
f32 = jnp.float32
MESH = pl.DeviceIdType.MESH


def rows_of(ref, first, stride):
    return ref[pl.ds(first, SUB, stride=stride), :]


def spread(ref, row):
    return jnp.broadcast_to(ref[pl.ds(row, 1), :], (SUB, LANES))


def filter_lanes(block, cols, filters):
    start = lax.axis_index("chan") * cols + block * LANES
    return pl.ds(pl.multiple_of(lax.rem(start, filters), LANES), LANES)


def block_lanes(block):
    return pl.ds(pl.multiple_of(block * LANES, LANES), LANES)


def tree(values):
    while len(values) > 1:
        values = [values[i] + values[i + 1] for i in range(0, len(values), 2)]
    return values[0]


def state_block(scale, block, fl, sig, gate, outer, cot, res, logr, g_s, w_s, a_s, h_s, pw_s, st, lag_s, xs, ys, edge,
                moment, gsum):
    rows = sig.shape[0]
    modes = res.shape[0]
    segs = rows // SEG
    groups = segs // SUB
    g_s[...] = (sig[...].astype(f32) * gate[...].astype(f32)).astype(jnp.bfloat16).astype(f32)
    w_s[...] = (cot[...].astype(f32) * outer[...].astype(f32)).astype(jnp.bfloat16).astype(f32)
    rate = jnp.exp(logr[:, fl])
    amp = res[:, fl] * scale
    a = jnp.exp(-rate)
    a_s[...] = a
    power = jnp.ones((modes, LANES), f32)
    for u in range(SEG):
        pw_s[u * modes : (u + 1) * modes, :] = power
        h_s[u : u + 1, :] = jnp.sum(amp * power, 0, keepdims=True)
        power = power * a
    seg_decay = power

    @pl.loop(0, groups)
    def _(group):
        base = group * (SUB * SEG)
        for half in range(0, modes, SUB):
            decay = [spread(a_s, half + k) for k in range(SUB)]
            zero = jnp.zeros((SUB, LANES), f32)
            x, z, y, v = ([zero] * SUB for _ in range(4))
            for j in range(SEG):
                gj = rows_of(g_s, base + j, SEG)
                wj = rows_of(w_s, base + SEG - 1 - j, SEG)
                for k in range(SUB):
                    x[k] = decay[k] * (x[k] + gj)
                    z[k] = decay[k] * z[k] + x[k]
                    t = decay[k] * y[k]
                    y[k] = t + wj
                    v[k] = decay[k] * v[k] + t
            for k in range(SUB):
                at = pl.ds(pl.multiple_of((half + k) * segs + group * SUB, SUB), SUB)
                st[0, at, :] = x[k]
                st[1, at, :] = z[k]
                st[2, at, :] = y[k]
                st[3, at, :] = v[k]
        g = [rows_of(g_s, base + j, SEG) for j in range(SEG)]
        w = [rows_of(w_s, base + j, SEG) for j in range(SEG)]
        for u in range(SEG):
            total = w[u] * g[0]
            for j in range(u + 1, SEG):
                total = total + w[j] * g[j - u]
            lag_s[pl.ds(pl.multiple_of((group * SEG + u) * SUB, SUB), SUB), :] = total

    gr = jnp.zeros((modes, LANES), f32)
    gl = jnp.zeros((modes, LANES), f32)
    for u in range(SEG):
        total = lag_s[u * SUB : (u + 1) * SUB, :]
        for group in range(1, groups):
            first = (group * SEG + u) * SUB
            total = total + lag_s[first : first + SUB, :]
        term = jnp.sum(total, 0, keepdims=True) * pw_s[u * modes : (u + 1) * modes, :]
        gr = gr + term
        if u > 0:
            gl = gl + float(u) * term
    x = jnp.zeros((modes, LANES), f32)
    xd = x
    for seg in range(segs):
        at = pl.ds(seg, modes, stride=segs)
        e, d, y, v = (st[i, at, :] for i in range(4))
        xs[seg * modes : (seg + 1) * modes, :] = x
        if seg > 0:
            gr = gr + x * y
            gl = gl + (xd * y + x * v)
        xd = seg_decay * (xd + float(SEG) * x) + d
        x = seg_decay * x + e
    y = jnp.zeros((modes, LANES), f32)
    yv = y
    for seg in reversed(range(segs)):
        at = pl.ds(seg, modes, stride=segs)
        ys[seg * modes : (seg + 1) * modes, :] = y
        yv = st[3, at, :] + seg_decay * (yv + float(SEG) * y)
        y = st[2, at, :] + seg_decay * y
    edge[0, block] = x
    edge[1, block] = y
    moment[0] = xd
    moment[1] = yv
    gsum[0] = gr
    gsum[1] = gl


def inner_block(rows, g_s, w_s, h_s, conv, grad):
    @pl.loop(0, rows // (SEG * SUB))
    def _(group):
        base = group * (SUB * SEG)
        h = [spread(h_s, u) for u in range(SEG)]
        g = [rows_of(g_s, base + j, SEG) for j in range(SEG)]
        for j in range(SEG):
            forward = h[0] * g[j]
            for u in range(1, j + 1):
                forward = forward + h[u] * g[j - u]
            conv[pl.ds(base + j, SUB, stride=SEG), :] = forward
        w = [rows_of(w_s, base + j, SEG) for j in range(SEG)]
        for j in range(SEG):
            backward = h[0] * w[j]
            for u in range(1, SEG - j):
                backward = backward + h[u] * w[j + u]
            grad[pl.ds(base + j, SUB, stride=SEG), :] = backward


def gradient_block(scale, parts, span, block, fl, edges, edge, moment, gsum, res, logr, totals, carry):
    place = lax.axis_index("seq")
    rate = jnp.exp(logr[:, fl])
    x0 = jnp.zeros(rate.shape, f32)
    xm = x0
    y0 = x0
    for other in range(parts):
        ahead = jnp.maximum(place - 1 - other, 0).astype(f32) * float(span)
        behind = jnp.maximum(other - place - 1, 0).astype(f32) * float(span)
        value = edges[other, block]
        e = jnp.where(other < place, value, 0.0) * jnp.exp(-rate * ahead)
        x0 = x0 + e
        xm = xm + ahead * e
        y0 = y0 + jnp.where(other > place, value, 0.0) * jnp.exp(-rate * behind)
    carry[0] = x0
    carry[1] = y0
    w = edge[1, block]
    gr = gsum[0] + x0 * w
    gl = gsum[1] + x0 * moment[1] + xm * w + moment[0] * y0
    totals[0, :, fl] = totals[0, :, fl] + scale * gr
    totals[1, :, fl] = totals[1, :, fl] - scale * (res[:, fl] * rate) * gl


def output_block(scale, fl, sig, gate, cot, res, logr, conv, grad, xs, ys, carry, out_sig, out_gate, out_outer,
                 a_s, p_s, q_s):
    rows = sig.shape[0]
    modes = res.shape[0]
    segs = rows // SEG
    rate = jnp.exp(logr[:, fl])
    amp = res[:, fl] * scale
    a_s[...] = jnp.exp(-rate)
    seg_decay = jnp.exp(-rate * float(SEG))
    p = amp * carry[0]
    q = amp * carry[1]
    for seg in range(segs):
        at = slice(seg * modes, (seg + 1) * modes)
        p_s[at, :] = amp * xs[at, :] + p
        p = p * seg_decay
        back = segs - 1 - seg
        at = slice(back * modes, (back + 1) * modes)
        q_s[at, :] = amp * ys[at, :] + q
        q = q * seg_decay

    @pl.loop(0, segs // SUB)
    def _(group):
        base = group * (SUB * SEG)
        for half in range(0, modes, SUB):
            decay = [spread(a_s, half + k) for k in range(SUB)]
            p = [rows_of(p_s, group * (SUB * modes) + half + k, modes) for k in range(SUB)]
            q = [rows_of(q_s, group * (SUB * modes) + half + k, modes) for k in range(SUB)]
            for j in range(SEG):
                at = pl.ds(base + j, SUB, stride=SEG)
                conv[at, :] = conv[at, :] + tree(p)
                q = [decay[k] * q[k] for k in range(SUB)]
                at = pl.ds(base + SEG - 1 - j, SUB, stride=SEG)
                grad[at, :] = grad[at, :] + tree(q)
                if j < SEG - 1:
                    p = [decay[k] * p[k] for k in range(SUB)]

    d = grad[...]
    out_sig[...] = (d * gate[...].astype(f32)).astype(jnp.bfloat16)
    out_gate[...] = (d * sig[...].astype(f32)).astype(jnp.bfloat16)
    out_outer[...] = (conv[...] * cot[...].astype(f32)).astype(jnp.bfloat16)


def whole_kernel(
    scale, norm, parts, groups_chan,
    sig_h, gate_h, outer_h, cot_h, res_h, logr_h,
    out_sig_h, out_gate_h, out_outer_h, out_res, out_rate,
    ins, params, outs, g_s, w_s, conv, grad, xs, ys, edge, edges, moment, gsum, carry, h_s,
    a_s, pw_s, st, lag_s, p_s, q_s, totals, pieces, landed, slots, final,
    in_sem, param_sem, out_sem, edge_send, edge_recv, rs_send, rs_recv, mid_send, mid_recv, end_send, end_recv,
):
    rows, cols = sig_h.shape
    modes, filters = res_h.shape
    blocks = cols // LANES
    place = lax.axis_index("seq")
    column = lax.axis_index("chan")
    barrier = pltpu.get_barrier_semaphore()

    def along(axis, index, size, d):
        return {axis: lax.rem(index + d, size)}

    def remote(src, dst, send, recv, device):
        return pltpu.make_async_remote_copy(
            src_ref=src, dst_ref=dst, send_sem=send, recv_sem=recv, device_id=device, device_id_type=MESH
        )

    for d in range(1, parts):
        pl.semaphore_signal(barrier, inc=1, device_id=along("seq", place, parts, d), device_id_type=MESH)
    for d in range(1, groups_chan):
        pl.semaphore_signal(barrier, inc=1, device_id=along("chan", column, groups_chan, d), device_id_type=MESH)

    param_copies = [
        pltpu.make_async_copy(ref, params.at[i], param_sem.at[i]) for i, ref in enumerate((res_h, logr_h))
    ]
    for copy in param_copies:
        copy.start()

    def fetch(i, ref, block):
        return pltpu.make_async_copy(ref.at[:, block_lanes(block)], ins.at[i, block], in_sem.at[i, block])

    whole_inputs = (sig_h, gate_h, outer_h, cot_h)

    @pl.loop(0, blocks)
    def _(block):
        for i, ref in enumerate(whole_inputs):
            fetch(i, ref, block).start()

    for copy in param_copies:
        copy.wait()
    pl.semaphore_wait(barrier, parts - 1 + groups_chan - 1)
    res, logr = params.at[0], params.at[1]

    def edge_copy(d, block):
        other = lax.rem(place + d, parts)
        which = jnp.where(other > place, 0, 1)
        if block is None:
            src, dst = edge.at[which], edges.at[place]
        else:
            src, dst = edge.at[which, block], edges.at[place, block]
        return remote(src, dst, edge_send.at[d], edge_recv.at[d], {"seq": other})

    @pl.loop(0, blocks)
    def _(block):
        for i, ref in enumerate(whole_inputs):
            fetch(i, ref, block).wait()
        sig, gate, outer, cot = (ins.at[i, block] for i in range(4))
        state_block(
            scale, block, filter_lanes(block, cols, filters), sig, gate, outer, cot, res, logr,
            g_s.at[block], w_s.at[block], a_s, h_s.at[block], pw_s, st, lag_s, xs.at[block], ys.at[block], edge,
            moment.at[block], gsum.at[block],
        )
        for d in range(1, parts):
            edge_copy(d, block).start()

    def inner(first, last):
        @pl.loop(first, last)
        def _(block):
            inner_block(rows, g_s.at[block], w_s.at[block], h_s.at[block], conv.at[block], grad.at[block])

    early = (blocks + 1) // 2
    inner(0, early)
    for d in range(1, parts):
        source = lax.rem(place + parts - d, parts)
        remote(edge.at[0], edges.at[source], edge_send.at[d], edge_recv.at[d], {"seq": source}).wait_recv()
    totals[...] = jnp.zeros_like(totals)
    edges[place] = jnp.zeros_like(edge[0])

    @pl.loop(0, blocks)
    def _(block):
        gradient_block(
            scale, parts, rows, block, filter_lanes(block, cols, filters), edges, edge, moment.at[block],
            gsum.at[block], res, logr, totals, carry.at[block],
        )

    size = 2 * modes // parts
    for p in range(parts):
        which, first = divmod(p * size, modes)
        pieces[p] = totals[which, first : first + size, :]

    def scatter(d):
        other = lax.rem(place + d, parts)
        return remote(pieces.at[other], landed.at[d], rs_send.at[d], rs_recv.at[d], {"seq": other})

    def middle(d):
        other = lax.rem(column + d, groups_chan)
        return remote(slots.at[column], slots.at[column], mid_send.at[d], mid_recv.at[d], {"chan": other})

    def middle_arrival(d):
        source = lax.rem(column + groups_chan - d, groups_chan)
        return remote(slots.at[source], slots.at[source], mid_send.at[d], mid_recv.at[d], {"chan": source})

    def ending(d):
        other = lax.rem(place + d, parts)
        return remote(final.at[place], final.at[place], end_send.at[d], end_recv.at[d], {"seq": other})

    def ending_arrival(d):
        source = lax.rem(place + parts - d, parts)
        return remote(final.at[source], final.at[source], end_send.at[d], end_recv.at[d], {"seq": source})

    for d in range(1, parts):
        scatter(d).start()
    inner(early, blocks)

    def put(i, ref, block):
        return pltpu.make_async_copy(outs.at[i, block], ref.at[:, block_lanes(block)], out_sem.at[i, block])

    whole_outputs = (out_sig_h, out_gate_h, out_outer_h)

    def outputs(first, last):
        if first == last:
            return

        @pl.loop(first, last)
        def _(block):
            output_block(
                scale, filter_lanes(block, cols, filters), ins.at[0, block], ins.at[1, block], ins.at[3, block],
                res, logr, conv.at[block], grad.at[block], xs.at[block], ys.at[block], carry.at[block],
                outs.at[0, block], outs.at[1, block], outs.at[2, block], a_s, p_s, q_s,
            )
            for i, ref in enumerate(whole_outputs):
                put(i, ref, block).start()

    first_stop = blocks // 8
    second_stop = blocks - blocks // 4
    outputs(0, first_stop)
    for d in range(1, parts):
        scatter(d).wait_recv()
    mine = pieces[place]
    for d in range(1, parts):
        mine = mine + landed[d]
    slots[column] = mine
    for d in range(1, groups_chan):
        middle(d).start()
    outputs(first_stop, second_stop)
    for d in range(1, groups_chan):
        middle_arrival(d).wait_recv()
    summed = slots[0]
    for other in range(1, groups_chan):
        summed = summed + slots[other]
    final[place] = norm * summed
    for d in range(1, parts):
        ending(d).start()
    outputs(second_stop, blocks)
    for d in range(1, parts):
        ending_arrival(d).wait_recv()
    for p in range(parts):
        which, first = divmod(p * size, modes)
        target = (out_res, out_rate)[which]
        target[first : first + size, :] = final[p]

    for d in range(1, parts):
        edge_copy(d, None).wait_send()
        scatter(d).wait_send()
        ending(d).wait_send()
    for d in range(1, groups_chan):
        middle(d).wait_send()

    @pl.loop(0, blocks)
    def _(block):
        for i, ref in enumerate(whole_outputs):
            put(i, ref, block).wait()


def on_device(signal_in, gate_in, outer_gate, cotangent, residues, log_rates):
    parts = lax.axis_size("seq")
    groups_chan = lax.axis_size("chan")
    rows, cols = signal_in.shape
    modes, filters = residues.shape
    total = parts * rows
    blocks = cols // LANES
    segs = rows // SEG
    groups = segs // SUB
    size = 2 * modes // parts
    scale = float(total) ** (-0.5)
    norm = float(total * cols * groups_chan // filters) ** (-0.5)
    whole = pl.BlockSpec(memory_space=pltpu.VMEM)
    far = pl.BlockSpec(memory_space=pl.ANY)
    shape = jax.ShapeDtypeStruct
    small = pltpu.VMEM((modes, LANES), f32)
    tiles = pltpu.VMEM((blocks, rows, LANES), f32)
    states = pltpu.VMEM((blocks, segs * modes, LANES), f32)
    pair = pltpu.VMEM((blocks, 2, modes, LANES), f32)
    dma = pltpu.SemaphoreType.DMA
    return pl.pallas_call(
        functools.partial(whole_kernel, scale, norm, parts, groups_chan),
        out_shape=(
            shape((rows, cols), jnp.bfloat16),
            shape((rows, cols), jnp.bfloat16),
            shape((rows, cols), jnp.bfloat16),
            shape((modes, filters), f32),
            shape((modes, filters), f32),
        ),
        in_specs=[pl.BlockSpec(memory_space=pltpu.HBM)] * 6,
        out_specs=(far, far, far, whole, whole),
        scratch_shapes=[
            pltpu.VMEM((4, blocks, rows, LANES), jnp.bfloat16),
            pltpu.VMEM((2, modes, filters), f32),
            pltpu.VMEM((3, blocks, rows, LANES), jnp.bfloat16),
            tiles,
            tiles,
            tiles,
            tiles,
            states,
            states,
            pltpu.VMEM((2, blocks, modes, LANES), f32),
            pltpu.VMEM((parts, blocks, modes, LANES), f32),
            pair,
            pair,
            pair,
            pltpu.VMEM((blocks, SEG, LANES), f32),
            small,
            pltpu.VMEM((SEG * modes, LANES), f32),
            pltpu.VMEM((4, modes * segs, LANES), f32),
            pltpu.VMEM((groups * SEG * SUB, LANES), f32),
            pltpu.VMEM((segs * modes, LANES), f32),
            pltpu.VMEM((segs * modes, LANES), f32),
            pltpu.VMEM((2, modes, filters), f32),
            pltpu.VMEM((parts, size, filters), f32),
            pltpu.VMEM((parts, size, filters), f32),
            pltpu.VMEM((groups_chan, size, filters), f32),
            pltpu.VMEM((parts, size, filters), f32),
            dma((4, blocks)),
            dma((2,)),
            dma((3, blocks)),
            dma((parts,)),
            dma((parts,)),
            dma((parts,)),
            dma((parts,)),
            dma((groups_chan,)),
            dma((groups_chan,)),
            dma((parts,)),
            dma((parts,)),
        ],
        compiler_params=pltpu.CompilerParams(
            vmem_limit_bytes=48 * 1024 * 1024, collective_id=0, has_side_effects=True
        ),
        name="whole",
    )(signal_in, gate_in, outer_gate, cotangent, residues, log_rates)


def solution(mesh):
    placed = (P("seq", "chan"), P("seq", "chan"), P("seq", "chan"), P("seq", "chan"), P(), P())
    return jax.shard_map(
        on_device,
        mesh=mesh,
        in_specs=placed,
        out_specs=(P("seq", "chan"), P("seq", "chan"), P("seq", "chan"), P(), P()),
        check_vma=False,
    )
```

time: 480 us -> 39 us (0.08)
  the two profiles are of different devices: /device:TPU:1 before, /device:TPU:0 now
where the time goes in v2:
time: 39 us; the launch traced here: 38.5 us
  Pallas kernels  28.6 us (73%)
  local copies, waits for them, and re-layouts  9.28 us (24%)
  between operations  0.66 us (2%)
    pallas_call x1, Pallas kernels, on_device(): pl.pallas_call(functools.partial(whole_kernel, scale, norm, parts, groups...  28.6 us
    unnamed x17, local copies, waits for them, and re-layouts  9.28 us

profile of v2, /device:TPU:0, one launch (start us, length us, event | category | flops | bytes accessed | tf_op | source)
XLA Modules:
  0.0 38.5 jit_solution(8829291161265034930)
XLA Ops:
  0.6 0.0 copy-start
  0.6 1.0 %copy-done = bf16[256,1024]{1,0:T(8,128)(2,1)S(1)} copy-done((bf16[256,1024]{1,0:T(8,128)(2,1)S(1)}, bf16[256,1024]{1,0:T(8,128)(2,1)}, u32[]{:S(2)}) %copy-start) | copy-done | bytes 524312
  1.7 0.0 copy-start.1
  1.7 1.0 %copy-done.1 = bf16[256,1024]{1,0:T(8,128)(2,1)S(1)} copy-done((bf16[256,1024]{1,0:T(8,128)(2,1)S(1)}, bf16[256,1024]{1,0:T(8,128)(2,1)}, u32[]{:S(2)}) %copy-start.1) | copy-done | bytes 524312
  2.7 0.0 copy-start.2
  2.7 1.0 %copy-done.2 = bf16[256,1024]{1,0:T(8,128)(2,1)S(1)} copy-done((bf16[256,1024]{1,0:T(8,128)(2,1)S(1)}, bf16[256,1024]{1,0:T(8,128)(2,1)}, u32[]{:S(2)}) %copy-start.2) | copy-done | bytes 524312
  3.8 0.0 copy-start.3
  3.8 1.0 %copy-done.3 = bf16[256,1024]{1,0:T(8,128)(2,1)S(1)} copy-done((bf16[256,1024]{1,0:T(8,128)(2,1)S(1)}, bf16[256,1024]{1,0:T(8,128)(2,1)}, u32[]{:S(2)}) %copy-start.3) | copy-done | bytes 524312
  4.8 0.0 copy-start.4
  4.8 0.8 %copy-done.4 = f32[16,512]{1,0:T(8,128)S(1)} copy-done((f32[16,512]{1,0:T(8,128)S(1)}, f32[16,512]{1,0:T(8,128)}, u32[]{:S(2)}) %copy-start.4) | copy-done | bytes 32792
  5.6 0.0 copy-start.5
  5.6 0.8 %copy-done.5 = f32[16,512]{1,0:T(8,128)S(1)} copy-done((f32[16,512]{1,0:T(8,128)S(1)}, f32[16,512]{1,0:T(8,128)}, u32[]{:S(2)}) %copy-start.5) | copy-done | bytes 32792
  6.3 28.6 %whole.1 = (bf16[256,1024]{1,0:T(8,128)(2,1)S(1)}, bf16[256,1024]{1,0:T(8,128)(2,1)S(1)}, bf16[256,1024]{1,0:T(8,128)(2,1)S(1)}, f32[16,512]{1,0:T(8,128)S(1)}, f32[16,512]{1,0:T(8,128)S(1)}) custom-call(bf16[256,1024]{1,0:T(8,128)(2,1)S(1)} %copy-done, bf16[256,1024]{1,0:T(8,128)(2,1)S(1)} %copy-done.1, bf16[256,1024]{1,0:T(8,128)(2,1)S(1)} %copy-done.2, ...), custom_call_target="tpu_custom_call" | custom-call | tf_op jit(solution)/shard_map/whole/pallas_call | solution.py:411
  34.9 0.8 %copy.16 = bf16[256,1024]{1,0:T(8,128)(2,1)} copy(bf16[256,1024]{1,0:T(8,128)(2,1)S(1)} %get-tuple-element.10) | data formatting | bytes 1048576
  35.7 0.8 %copy.17 = bf16[256,1024]{1,0:T(8,128)(2,1)} copy(bf16[256,1024]{1,0:T(8,128)(2,1)S(1)} %get-tuple-element.11) | data formatting | bytes 1048576
  36.5 0.8 %copy.18 = bf16[256,1024]{1,0:T(8,128)(2,1)} copy(bf16[256,1024]{1,0:T(8,128)(2,1)S(1)} %get-tuple-element.12) | data formatting | bytes 1048576
  37.3 0.6 %copy.19 = f32[16,512]{1,0:T(8,128)} copy(f32[16,512]{1,0:T(8,128)S(1)} %get-tuple-element.13) | data formatting | bytes 65536
  37.9 0.6 %copy.20 = f32[16,512]{1,0:T(8,128)} copy(f32[16,512]{1,0:T(8,128)S(1)} %get-tuple-element.14) | data formatting | bytes 65536
Async XLA Ops:
  0.6 1.0 %copy-start = (bf16[256,1024]{1,0:T(8,128)(2,1)S(1)}, bf16[256,1024]{1,0:T(8,128)(2,1)}, u32[]{:S(2)}) copy-start(bf16[256,1024]{1,0:T(8,128)(2,1)} %sig_h.1) | copy-start | bytes 1572868
  1.7 1.0 %copy-start.1 = (bf16[256,1024]{1,0:T(8,128)(2,1)S(1)}, bf16[256,1024]{1,0:T(8,128)(2,1)}, u32[]{:S(2)}) copy-start(bf16[256,1024]{1,0:T(8,128)(2,1)} %gate_h.1) | copy-start | bytes 1572868
  2.7 1.0 %copy-start.2 = (bf16[256,1024]{1,0:T(8,128)(2,1)S(1)}, bf16[256,1024]{1,0:T(8,128)(2,1)}, u32[]{:S(2)}) copy-start(bf16[256,1024]{1,0:T(8,128)(2,1)} %outer_h.1) | copy-start | bytes 1572868
  3.8 1.0 %copy-start.3 = (bf16[256,1024]{1,0:T(8,128)(2,1)S(1)}, bf16[256,1024]{1,0:T(8,128)(2,1)}, u32[]{:S(2)}) copy-start(bf16[256,1024]{1,0:T(8,128)(2,1)} %cot_h.1) | copy-start | bytes 1572868
  4.8 0.8 %copy-start.4 = (f32[16,512]{1,0:T(8,128)S(1)}, f32[16,512]{1,0:T(8,128)}, u32[]{:S(2)}) copy-start(f32[16,512]{1,0:T(8,128)} %res_h.1) | copy-start | bytes 98308
  5.6 0.8 %copy-start.5 = (f32[16,512]{1,0:T(8,128)S(1)}, f32[16,512]{1,0:T(8,128)}, u32[]{:S(2)}) copy-start(f32[16,512]{1,0:T(8,128)} %logr_h.1) | copy-start | bytes 98308

commit v3 on v2

--- a/solution.py
+++ b/solution.py
@@ -166,9 +166,8 @@
     totals[1, :, fl] = totals[1, :, fl] - scale * (res[:, fl] * rate) * gl
 
 
-def output_block(scale, fl, sig, gate, cot, res, logr, conv, grad, xs, ys, carry, out_sig, out_gate, out_outer,
-                 a_s, p_s, q_s):
-    rows = sig.shape[0]
+def output_block(scale, fl, res, logr, conv, grad, xs, ys, carry, a_s, p_s, q_s):
+    rows = conv.shape[0]
     modes = res.shape[0]
     segs = rows // SEG
     rate = jnp.exp(logr[:, fl])
@@ -202,17 +201,12 @@
                 if j < SEG - 1:
                     p = [decay[k] * p[k] for k in range(SUB)]
 
-    d = grad[...]
-    out_sig[...] = (d * gate[...].astype(f32)).astype(jnp.bfloat16)
-    out_gate[...] = (d * sig[...].astype(f32)).astype(jnp.bfloat16)
-    out_outer[...] = (conv[...] * cot[...].astype(f32)).astype(jnp.bfloat16)
-
 
 def whole_kernel(
     scale, norm, parts, groups_chan,
     sig_h, gate_h, outer_h, cot_h, res_h, logr_h,
-    out_sig_h, out_gate_h, out_outer_h, out_res, out_rate,
-    ins, params, outs, g_s, w_s, conv, grad, xs, ys, edge, edges, moment, gsum, carry, h_s,
+    conv_h, grad_h, sums_h,
+    ins, params, g_s, w_s, conv, grad, xs, ys, edge, edges, moment, gsum, carry, h_s,
     a_s, pw_s, st, lag_s, p_s, q_s, totals, pieces, landed, slots, final,
     in_sem, param_sem, out_sem, edge_send, edge_recv, rs_send, rs_recv, mid_send, mid_recv, end_send, end_recv,
 ):
@@ -221,20 +215,30 @@
     blocks = cols // LANES
     place = lax.axis_index("seq")
     column = lax.axis_index("chan")
+    pairs = pair_size(groups_chan)
     barrier = pltpu.get_barrier_semaphore()
-
-    def along(axis, index, size, d):
-        return {axis: lax.rem(index + d, size)}
 
     def remote(src, dst, send, recv, device):
         return pltpu.make_async_remote_copy(
             src_ref=src, dst_ref=dst, send_sem=send, recv_sem=recv, device_id=device, device_id_type=MESH
         )
 
-    for d in range(1, parts):
-        pl.semaphore_signal(barrier, inc=1, device_id=along("seq", place, parts, d), device_id_type=MESH)
-    for d in range(1, groups_chan):
-        pl.semaphore_signal(barrier, inc=1, device_id=along("chan", column, groups_chan, d), device_id_type=MESH)
+    low = lax.rem(column, pairs)
+    high = column // pairs
+    upper = groups_chan // pairs
+    team = parts * pairs
+    member = place * pairs + low
+
+    def mate(index):
+        return {"seq": index // pairs, "chan": high * pairs + lax.rem(index, pairs)}
+
+    def tower(index):
+        return {"chan": index * pairs + low}
+
+    for d in range(1, team):
+        pl.semaphore_signal(barrier, inc=1, device_id=mate(lax.rem(member + d, team)), device_id_type=MESH)
+    for d in range(1, upper):
+        pl.semaphore_signal(barrier, inc=1, device_id=tower(lax.rem(high + d, upper)), device_id_type=MESH)
 
     param_copies = [
         pltpu.make_async_copy(ref, params.at[i], param_sem.at[i]) for i, ref in enumerate((res_h, logr_h))
@@ -254,7 +258,7 @@
 
     for copy in param_copies:
         copy.wait()
-    pl.semaphore_wait(barrier, parts - 1 + groups_chan - 1)
+    pl.semaphore_wait(barrier, team - 1 + upper - 1)
     res, logr = params.at[0], params.at[1]
 
     def edge_copy(d, block):
@@ -299,39 +303,32 @@
             gsum.at[block], res, logr, totals, carry.at[block],
         )
 
-    size = 2 * modes // parts
-    for p in range(parts):
+    size = 2 * modes // team
+    for p in range(team):
         which, first = divmod(p * size, modes)
         pieces[p] = totals[which, first : first + size, :]
 
     def scatter(d):
-        other = lax.rem(place + d, parts)
-        return remote(pieces.at[other], landed.at[d], rs_send.at[d], rs_recv.at[d], {"seq": other})
-
-    def middle(d):
-        other = lax.rem(column + d, groups_chan)
-        return remote(slots.at[column], slots.at[column], mid_send.at[d], mid_recv.at[d], {"chan": other})
-
-    def middle_arrival(d):
-        source = lax.rem(column + groups_chan - d, groups_chan)
-        return remote(slots.at[source], slots.at[source], mid_send.at[d], mid_recv.at[d], {"chan": source})
-
-    def ending(d):
-        other = lax.rem(place + d, parts)
-        return remote(final.at[place], final.at[place], end_send.at[d], end_recv.at[d], {"seq": other})
-
-    def ending_arrival(d):
-        source = lax.rem(place + parts - d, parts)
-        return remote(final.at[source], final.at[source], end_send.at[d], end_recv.at[d], {"seq": source})
-
-    for d in range(1, parts):
+        other = lax.rem(member + d, team)
+        return remote(pieces.at[other], landed.at[d], rs_send.at[d], rs_recv.at[d], mate(other))
+
+    def middle(d, back=False):
+        other = lax.rem(high + (upper - d if back else d), upper)
+        slot = slots.at[other if back else high]
+        return remote(slot, slot, mid_send.at[d], mid_recv.at[d], tower(other))
+
+    def ending(d, back=False):
+        other = lax.rem(member + (team - d if back else d), team)
+        slot = final.at[other if back else member]
+        return remote(slot, slot, end_send.at[d], end_recv.at[d], mate(other))
+
+    for d in range(1, team):
         scatter(d).start()
     inner(early, blocks)
 
-    def put(i, ref, block):
-        return pltpu.make_async_copy(outs.at[i, block], ref.at[:, block_lanes(block)], out_sem.at[i, block])
-
-    whole_outputs = (out_sig_h, out_gate_h, out_outer_h)
+    def put(i, block):
+        src, dst = ((conv, conv_h), (grad, grad_h))[i]
+        return pltpu.make_async_copy(src.at[block], dst.at[:, block_lanes(block)], out_sem.at[i, block])
 
     def outputs(first, last):
         if first == last:
@@ -340,52 +337,64 @@
         @pl.loop(first, last)
         def _(block):
             output_block(
-                scale, filter_lanes(block, cols, filters), ins.at[0, block], ins.at[1, block], ins.at[3, block],
-                res, logr, conv.at[block], grad.at[block], xs.at[block], ys.at[block], carry.at[block],
-                outs.at[0, block], outs.at[1, block], outs.at[2, block], a_s, p_s, q_s,
+                scale, filter_lanes(block, cols, filters), res, logr, conv.at[block], grad.at[block], xs.at[block],
+                ys.at[block], carry.at[block], a_s, p_s, q_s,
             )
-            for i, ref in enumerate(whole_outputs):
-                put(i, ref, block).start()
+            for i in range(2):
+                put(i, block).start()
 
     first_stop = blocks // 8
     second_stop = blocks - blocks // 4
     outputs(0, first_stop)
-    for d in range(1, parts):
+    for d in range(1, team):
         scatter(d).wait_recv()
-    mine = pieces[place]
-    for d in range(1, parts):
+    mine = pieces[member]
+    for d in range(1, team):
         mine = mine + landed[d]
-    slots[column] = mine
-    for d in range(1, groups_chan):
+    slots[high] = mine
+    for d in range(1, upper):
         middle(d).start()
     outputs(first_stop, second_stop)
-    for d in range(1, groups_chan):
-        middle_arrival(d).wait_recv()
+    for d in range(1, upper):
+        middle(d, back=True).wait_recv()
     summed = slots[0]
-    for other in range(1, groups_chan):
+    for other in range(1, upper):
         summed = summed + slots[other]
-    final[place] = norm * summed
-    for d in range(1, parts):
+    final[member] = norm * summed
+    for d in range(1, team):
         ending(d).start()
     outputs(second_stop, blocks)
-    for d in range(1, parts):
-        ending_arrival(d).wait_recv()
-    for p in range(parts):
+    for d in range(1, team):
+        ending(d, back=True).wait_recv()
+    for p in range(team):
         which, first = divmod(p * size, modes)
-        target = (out_res, out_rate)[which]
-        target[first : first + size, :] = final[p]
+        sums_h[which, first : first + size, :] = final[p]
 
     for d in range(1, parts):
         edge_copy(d, None).wait_send()
+    for d in range(1, team):
         scatter(d).wait_send()
         ending(d).wait_send()
-    for d in range(1, groups_chan):
+    for d in range(1, upper):
         middle(d).wait_send()
 
     @pl.loop(0, blocks)
     def _(block):
-        for i, ref in enumerate(whole_outputs):
-            put(i, ref, block).wait()
+        for i in range(2):
+            put(i, block).wait()
+
+
+def gate_kernel(conv, grad, sig, gate, cot, sums, out_sig, out_gate, out_outer, out_res, out_rate):
+    d = grad[...]
+    out_sig[...] = (d * gate[...].astype(f32)).astype(jnp.bfloat16)
+    out_gate[...] = (d * sig[...].astype(f32)).astype(jnp.bfloat16)
+    out_outer[...] = (conv[...] * cot[...].astype(f32)).astype(jnp.bfloat16)
+    out_res[...] = sums[0]
+    out_rate[...] = sums[1]
+
+
+def pair_size(columns):
+    return 2 if columns % 2 == 0 else 1
 
 
 def on_device(signal_in, gate_in, outer_gate, cotangent, residues, log_rates):
@@ -397,7 +406,10 @@
     blocks = cols // LANES
     segs = rows // SEG
     groups = segs // SUB
-    size = 2 * modes // parts
+    pairs = pair_size(groups_chan)
+    team = parts * pairs
+    upper = groups_chan // pairs
+    size = 2 * modes // team
     scale = float(total) ** (-0.5)
     norm = float(total * cols * groups_chan // filters) ** (-0.5)
     whole = pl.BlockSpec(memory_space=pltpu.VMEM)
@@ -408,21 +420,18 @@
     states = pltpu.VMEM((blocks, segs * modes, LANES), f32)
     pair = pltpu.VMEM((blocks, 2, modes, LANES), f32)
     dma = pltpu.SemaphoreType.DMA
-    return pl.pallas_call(
+    conv, grad, sums = pl.pallas_call(
         functools.partial(whole_kernel, scale, norm, parts, groups_chan),
         out_shape=(
-            shape((rows, cols), jnp.bfloat16),
-            shape((rows, cols), jnp.bfloat16),
-            shape((rows, cols), jnp.bfloat16),
-            shape((modes, filters), f32),
-            shape((modes, filters), f32),
+            shape((rows, cols), f32),
+            shape((rows, cols), f32),
+            shape((2, modes, filters), f32),
         ),
         in_specs=[pl.BlockSpec(memory_space=pltpu.HBM)] * 6,
-        out_specs=(far, far, far, whole, whole),
+        out_specs=(far, far, whole),
         scratch_shapes=[
             pltpu.VMEM((4, blocks, rows, LANES), jnp.bfloat16),
             pltpu.VMEM((2, modes, filters), f32),
-            pltpu.VMEM((3, blocks, rows, LANES), jnp.bfloat16),
             tiles,
             tiles,
             tiles,
@@ -442,27 +451,40 @@
             pltpu.VMEM((segs * modes, LANES), f32),
             pltpu.VMEM((segs * modes, LANES), f32),
             pltpu.VMEM((2, modes, filters), f32),
-            pltpu.VMEM((parts, size, filters), f32),
-            pltpu.VMEM((parts, size, filters), f32),
-            pltpu.VMEM((groups_chan, size, filters), f32),
-            pltpu.VMEM((parts, size, filters), f32),
+            pltpu.VMEM((team, size, filters), f32),
+            pltpu.VMEM((team, size, filters), f32),
+            pltpu.VMEM((upper, size, filters), f32),
+            pltpu.VMEM((team, size, filters), f32),
             dma((4, blocks)),
             dma((2,)),
-            dma((3, blocks)),
+            dma((2, blocks)),
             dma((parts,)),
             dma((parts,)),
-            dma((parts,)),
-            dma((parts,)),
-            dma((groups_chan,)),
-            dma((groups_chan,)),
-            dma((parts,)),
-            dma((parts,)),
+            dma((team,)),
+            dma((team,)),
+            dma((upper,)),
+            dma((upper,)),
+            dma((team,)),
+            dma((team,)),
         ],
         compiler_params=pltpu.CompilerParams(
-            vmem_limit_bytes=48 * 1024 * 1024, collective_id=0, has_side_effects=True
+            collective_id=0, has_side_effects=True
         ),
         name="whole",
     )(signal_in, gate_in, outer_gate, cotangent, residues, log_rates)
+    steps = 4 if blocks % 4 == 0 else 1
+    tile = pl.BlockSpec((rows, cols // steps), lambda i: (0, i))
+    both = pl.BlockSpec((2, modes, filters), lambda i: (0, 0, 0))
+    one = pl.BlockSpec((modes, filters), lambda i: (0, 0))
+    narrow = shape((rows, cols), jnp.bfloat16)
+    return pl.pallas_call(
+        gate_kernel,
+        out_shape=(narrow, narrow, narrow, shape((modes, filters), f32), shape((modes, filters), f32)),
+        grid=(steps,),
+        in_specs=[tile] * 5 + [both],
+        out_specs=(tile, tile, tile, one, one),
+        name="gates",
+    )(conv, grad, signal_in, gate_in, cotangent, sums)
 
 
 def solution(mesh):

time: 39 us -> 34.1 us (0.87)
  local copies, waits for them, and re-layouts: 9.28 us -> 0 us
  Pallas kernels: 28.6 us -> 33.2 us
    unnamed x17 -> x0, local copies, waits for them, and re-layouts: 9.28 us -> none
    pallas_call x0 -> x1, Pallas kernels: none -> 4.16 us  [on_device(): pl.pallas_call(gate_kernel, out_shape=(narrow, narrow, narrow, shape((mod...]
    pallas_call x1, Pallas kernels: 28.6 us -> 29.1 us  [on_device(): pl.pallas_call(functools.partial(whole_kernel, scale, norm, parts, groups...]
where the time goes in v3:
time: 34.1 us; the launch traced here: 33.9 us
  Pallas kernels  33.2 us (97%)
  between operations  0.64 us (2%)
    pallas_call x1, Pallas kernels, on_device(): pl.pallas_call(functools.partial(whole_kernel, scale, norm, parts, groups...  29.1 us
    pallas_call x1, Pallas kernels, on_device(): pl.pallas_call(gate_kernel, out_shape=(narrow, narrow, narrow, shape((mod...  4.16 us

profile of v3, /device:TPU:0, one launch (start us, length us, event | category | flops | bytes accessed | tf_op | source)
XLA Modules:
  0.0 33.9 jit_solution(1035826296155328459)
XLA Ops:
  0.6 29.1 %whole.1 = (f32[256,1024]{1,0:T(8,128)}, f32[256,1024]{1,0:T(8,128)}, f32[2,16,512]{2,1,0:T(8,128)}) custom-call(bf16[256,1024]{1,0:T(8,128)(2,1)} %sig.1, bf16[256,1024]{1,0:T(8,128)(2,1)} %gate.1, bf16[256,1024]{1,0:T(8,128)(2,1)} %outer_h.1, bf16[256,1024]{1,0:T(8,128)(2,1)} %cot.1, f32[16,512]{1,0:T(8,128)} %res_h.1, f32[16,512]{1,0:T(8,128)} %logr_h.1), custom_call_target="tpu_custom_call" | custom-call | tf_op jit(solution)/shard_map/whole/pallas_call | solution.py:423
  29.7 4.2 %gates.1 = (bf16[256,1024]{1,0:T(8,128)(2,1)}, bf16[256,1024]{1,0:T(8,128)(2,1)}, bf16[256,1024]{1,0:T(8,128)(2,1)}, f32[16,512]{1,0:T(8,128)}, f32[16,512]{1,0:T(8,128)}) custom-call(f32[256,1024]{1,0:T(8,128)} %get-tuple-element.8.conv, f32[256,1024]{1,0:T(8,128)} %get-tuple-element.9.grad, bf16[256,1024]{1,0:T(8,128)(2,1)} %sig.1, ...), custom_call_target="tpu_custom_call" | custom-call | tf_op jit(solution)/shard_map/gates/pallas_call | solution.py:480

commit v4 on v3

--- a/solution.py
+++ b/solution.py
@@ -205,8 +205,8 @@
 def whole_kernel(
     scale, norm, parts, groups_chan,
     sig_h, gate_h, outer_h, cot_h, res_h, logr_h,
-    conv_h, grad_h, sums_h,
-    ins, params, g_s, w_s, conv, grad, xs, ys, edge, edges, moment, gsum, carry, h_s,
+    out_sig_h, out_gate_h, out_outer_h, sums_h,
+    ins, params, outs, g_s, w_s, conv, grad, xs, ys, edge, edges, moment, gsum, carry, h_s,
     a_s, pw_s, st, lag_s, p_s, q_s, totals, pieces, landed, slots, final,
     in_sem, param_sem, out_sem, edge_send, edge_recv, rs_send, rs_recv, mid_send, mid_recv, end_send, end_recv,
 ):
@@ -327,8 +327,8 @@
     inner(early, blocks)
 
     def put(i, block):
-        src, dst = ((conv, conv_h), (grad, grad_h))[i]
-        return pltpu.make_async_copy(src.at[block], dst.at[:, block_lanes(block)], out_sem.at[i, block])
+        target = (out_sig_h, out_gate_h, out_outer_h)[i]
+        return pltpu.make_async_copy(outs.at[i, block], target.at[:, block_lanes(block)], out_sem.at[i, block])
 
     def outputs(first, last):
         if first == last:
@@ -340,7 +340,11 @@
                 scale, filter_lanes(block, cols, filters), res, logr, conv.at[block], grad.at[block], xs.at[block],
                 ys.at[block], carry.at[block], a_s, p_s, q_s,
             )
-            for i in range(2):
+            d = grad[block]
+            outs[0, block] = (d * ins[1, block].astype(f32)).astype(jnp.bfloat16)
+            outs[1, block] = (d * ins[0, block].astype(f32)).astype(jnp.bfloat16)
+            outs[2, block] = (conv[block] * ins[3, block].astype(f32)).astype(jnp.bfloat16)
+            for i in range(3):
                 put(i, block).start()
 
     first_stop = blocks // 8
@@ -380,17 +384,28 @@
 
     @pl.loop(0, blocks)
     def _(block):
-        for i in range(2):
+        for i in range(3):
             put(i, block).wait()
 
 
-def gate_kernel(conv, grad, sig, gate, cot, sums, out_sig, out_gate, out_outer, out_res, out_rate):
-    d = grad[...]
-    out_sig[...] = (d * gate[...].astype(f32)).astype(jnp.bfloat16)
-    out_gate[...] = (d * sig[...].astype(f32)).astype(jnp.bfloat16)
-    out_outer[...] = (conv[...] * cot[...].astype(f32)).astype(jnp.bfloat16)
-    out_res[...] = sums[0]
-    out_rate[...] = sums[1]
+def pass_kernel(sig, gate, outer, sums, out_sig, out_gate, out_outer, out_res, out_rate, held, sums_held, sem_in, sem_out):
+    chunks, depth = held.shape[1:3]
+    todo = []
+    for i, (src, dst) in enumerate(((sig, out_sig), (gate, out_gate), (outer, out_outer))):
+        for c in range(chunks):
+            at = pl.ds(c * depth, depth)
+            todo.append((src.at[at, :], held.at[i, c], dst.at[at, :]))
+    for i, dst in enumerate((out_res, out_rate)):
+        todo.append((sums.at[i], sums_held.at[i], dst))
+    into = [pltpu.make_async_copy(src, mid, sem_in.at[n]) for n, (src, mid, _) in enumerate(todo)]
+    out = [pltpu.make_async_copy(mid, dst, sem_out.at[n]) for n, (_, mid, dst) in enumerate(todo)]
+    for copy in into:
+        copy.start()
+    for first, second in zip(into, out):
+        first.wait()
+        second.start()
+    for copy in out:
+        copy.wait()
 
 
 def pair_size(columns):
@@ -420,18 +435,21 @@
     states = pltpu.VMEM((blocks, segs * modes, LANES), f32)
     pair = pltpu.VMEM((blocks, 2, modes, LANES), f32)
     dma = pltpu.SemaphoreType.DMA
-    conv, grad, sums = pl.pallas_call(
+    narrow = shape((rows, cols), jnp.bfloat16)
+    *products, sums = pl.pallas_call(
         functools.partial(whole_kernel, scale, norm, parts, groups_chan),
         out_shape=(
-            shape((rows, cols), f32),
-            shape((rows, cols), f32),
+            narrow,
+            narrow,
+            narrow,
             shape((2, modes, filters), f32),
         ),
         in_specs=[pl.BlockSpec(memory_space=pltpu.HBM)] * 6,
-        out_specs=(far, far, whole),
+        out_specs=(far, far, far, whole),
         scratch_shapes=[
             pltpu.VMEM((4, blocks, rows, LANES), jnp.bfloat16),
             pltpu.VMEM((2, modes, filters), f32),
+            pltpu.VMEM((3, blocks, rows, LANES), jnp.bfloat16),
             tiles,
             tiles,
             tiles,
@@ -457,7 +475,7 @@
             pltpu.VMEM((team, size, filters), f32),
             dma((4, blocks)),
             dma((2,)),
-            dma((2, blocks)),
+            dma((3, blocks)),
             dma((parts,)),
             dma((parts,)),
             dma((team,)),
@@ -472,19 +490,20 @@
         ),
         name="whole",
     )(signal_in, gate_in, outer_gate, cotangent, residues, log_rates)
-    steps = 4 if blocks % 4 == 0 else 1
-    tile = pl.BlockSpec((rows, cols // steps), lambda i: (0, i))
-    both = pl.BlockSpec((2, modes, filters), lambda i: (0, 0, 0))
-    one = pl.BlockSpec((modes, filters), lambda i: (0, 0))
-    narrow = shape((rows, cols), jnp.bfloat16)
+    chunks = 2
     return pl.pallas_call(
-        gate_kernel,
+        pass_kernel,
         out_shape=(narrow, narrow, narrow, shape((modes, filters), f32), shape((modes, filters), f32)),
-        grid=(steps,),
-        in_specs=[tile] * 5 + [both],
-        out_specs=(tile, tile, tile, one, one),
-        name="gates",
-    )(conv, grad, signal_in, gate_in, cotangent, sums)
+        in_specs=[far] * 4,
+        out_specs=(far,) * 5,
+        scratch_shapes=[
+            pltpu.VMEM((3, chunks, rows // chunks, cols), jnp.bfloat16),
+            pltpu.VMEM((2, modes, filters), f32),
+            dma((3 * chunks + 2,)),
+            dma((3 * chunks + 2,)),
+        ],
+        name="passed",
+    )(*products, sums)
 
 
 def solution(mesh):

time: 34.1 us -> 32.2 us (0.944)
  Pallas kernels: 33.2 us -> 31.4 us
    pallas_call x1, Pallas kernels: 4.16 us -> 2.23 us  [on_device(): pl.pallas_call(pass_kernel, out_shape=(narrow, narrow, narrow, shape((mod...]
where the time goes in v4:
time: 32.2 us; the launch traced here: 32 us
  Pallas kernels  31.4 us (98%)
  between operations  0.64 us (2%)
    pallas_call x1, Pallas kernels, on_device(): pl.pallas_call(functools.partial(whole_kernel, scale, norm, parts, groups...  29.1 us
    pallas_call x1, Pallas kernels, on_device(): pl.pallas_call(pass_kernel, out_shape=(narrow, narrow, narrow, shape((mod...  2.23 us

profile of v4, /device:TPU:0, one launch (start us, length us, event | category | flops | bytes accessed | tf_op | source)
XLA Modules:
  0.0 32.0 jit_solution(2389705340510823806)
XLA Ops:
  0.6 29.1 %whole.1 = (bf16[256,1024]{1,0:T(8,128)(2,1)}, bf16[256,1024]{1,0:T(8,128)(2,1)}, bf16[256,1024]{1,0:T(8,128)(2,1)}, f32[2,16,512]{2,1,0:T(8,128)}) custom-call(bf16[256,1024]{1,0:T(8,128)(2,1)} %sig_h.1, bf16[256,1024]{1,0:T(8,128)(2,1)} %gate_h.1, bf16[256,1024]{1,0:T(8,128)(2,1)} %outer_h.1, bf16[256,1024]{1,0:T(8,128)(2,1)} %cot_h.1, f32[16,512]{1,0:T(8,128)} %res_h.1, ...), custom_call_target="tpu_custom_call" | custom-call | tf_op jit(solution)/shard_map/whole/pallas_call | solution.py:439
  29.8 2.2 %passed.1 = (bf16[256,1024]{1,0:T(8,128)(2,1)}, bf16[256,1024]{1,0:T(8,128)(2,1)}, bf16[256,1024]{1,0:T(8,128)(2,1)}, f32[16,512]{1,0:T(8,128)}, f32[16,512]{1,0:T(8,128)}) custom-call(bf16[256,1024]{1,0:T(8,128)(2,1)} %get-tuple-element.9.sig, bf16[256,1024]{1,0:T(8,128)(2,1)} %get-tuple-element.10.gate, bf16[256,1024]{1,0:T(8,128)(2,1)} %get-tuple-element.11.outer, ...), custom_call_target="tpu_custom_call" | custom-call | tf_op jit(solution)/shard_map/passed/pallas_call | solution.py:494
